TPU v7x, 32 devices: a whole 2x2x4 slice. The times are simulated.
32 devices in a mesh: gx: 4 (over z), gy: 4 (over x, core), gz: 2 (over y).
Axes of the slice: x: 2, y: 2, z: 4, core: 2. Of those that a mesh axis runs over, the one named last changes fastest.
Arguments:
- activations: bfloat16 [1024, 8192], P('gy', 'gx'), may hold values from -0.5 to 0.5
- cotangent: bfloat16 [1024, 8192], P('gy', 'gx'), may hold values from -1.5 to 1.5
- gate_pre: bfloat16 [1024, 26624], P('gx', ('gy', 'gz')), may hold values from -6 to 6
- up_pre: bfloat16 [1024, 26624], P('gx', ('gy', 'gz')), may hold values from -6 to 6
- gate_weight: bfloat16 [8192, 26624], P('gx', ('gy', 'gz')), may hold values from -0.0625 to 0.0625
- up_weight: bfloat16 [8192, 26624], P('gx', ('gy', 'gz')), may hold values from -0.0625 to 0.0625
- down_weight: bfloat16 [26624, 8192], P(('gy', 'gz'), 'gx'), may hold values from -0.15625 to 0.15625
Outputs:
- input_grad: bfloat16 [1024, 8192], P('gy', 'gx')
- gate_grad: bfloat16 [8192, 26624], P('gx', ('gy', 'gz'))
- up_grad: bfloat16 [8192, 26624], P('gx', ('gy', 'gz'))
- down_grad: bfloat16 [26624, 8192], P(('gy', 'gz'), 'gx')
All inputs are finite; a program needn't handle non-finite values.
Results may differ from a plain program's by a relative error of at most 0.015.
Values may be sent and summed in bfloat16 or wider, within the bound.
A program may use at most 192 MiB of HBM per device.

v0:
```python
import jax
import jax.numpy as jnp
from jax import lax
from jax.sharding import PartitionSpec as P

over_rows = (((0,), (0,)), ((), ()))
over_cols = (((1,), (1,)), ((), ()))
BF = jnp.bfloat16
F32 = jnp.float32


def swiglu_grads(gate_in, up_in, grad_hidden):
    gate_val = gate_in.astype(F32)
    up_val = up_in.astype(F32)
    grad_hidden = grad_hidden.astype(F32)
    sigmoid = jax.nn.sigmoid(gate_val)
    hidden = (gate_val * sigmoid * up_val).astype(BF)
    grad_gate = (grad_hidden * up_val * sigmoid * (1.0 + gate_val * (1.0 - sigmoid))).astype(BF)
    grad_up = (grad_hidden * gate_val * sigmoid).astype(BF)
    return (hidden, grad_gate, grad_up)


def after(value, earlier):
    seen = earlier.reshape(-1)[0].astype(F32)
    return value + jnp.minimum(jnp.abs(seen), 0.0).astype(value.dtype)


def line_gather(block, axis, n):
    me = lax.axis_index(axis)
    right, left = ({}, {})
    from_left = from_right = block
    for s in range(1, n):
        from_left = lax.ppermute(from_left, axis, [(i, i + 1) for i in range(s - 1, n - 1)])
        from_right = lax.ppermute(from_right, axis, [(i, i - 1) for i in range(1, n - s + 1)])
        right[s], left[s] = (from_left, from_right)
    return [block] + [jnp.where(me >= r, right[r], left[n - r]) for r in range(1, n)]


def line_scatter(part, axis, n):
    right = left = None
    for t in range(1, n):
        to_right, to_left = (part(n - t), part(t))
        if right is not None:
            to_right = to_right + right.astype(F32)
            to_left = to_left + left.astype(F32)
        right = lax.ppermute(to_right.astype(BF), axis, [(i, i + 1) for i in range(min(t, n - 1))])
        left = lax.ppermute(to_left.astype(BF), axis, [(i, i - 1) for i in range(max(n - t, 1), n)])
    total = part(0)
    if right is not None:
        total = total + right.astype(F32) + left.astype(F32)
    return total


def pair_scatter(total, axis, n):
    me = lax.axis_index(axis)
    if n & n - 1:
        return lax.psum_scatter(total, axis, scatter_dimension=0, tiled=False)
    stride = 1
    while stride < n:
        pairs = total.reshape((total.shape[0] // 2, 2) + total.shape[1:])
        bit = me // stride % 2
        mine = lax.dynamic_index_in_dim(pairs, bit, 1, keepdims=False)
        theirs = lax.dynamic_index_in_dim(pairs, 1 - bit, 1, keepdims=False)
        got = lax.ppermute(theirs.astype(BF), axis, [(i, i ^ stride) for i in range(n)])
        total = mine + got.astype(F32)
        stride *= 2
    return total[0]


def chunks_of(width):
    tile = 256 if width % 256 == 0 else 64
    units = width // tile
    if width < 2048:
        return [(0, width)]
    sizes = [(units * 5 + 6) // 13, (units * 5 + 6) // 13]
    sizes.append(units - sum(sizes))
    out, at = ([], 0)
    for size in sizes:
        out.append((at * tile, size * tile))
        at += size
    return out


def shards(activations, cotangent, gate_pre, up_pre, gate_weight, up_weight, down_weight):
    n, ny, nz = (lax.axis_size("gx"), lax.axis_size("gy"), lax.axis_size("gz"))
    me = lax.axis_index("gx")
    rows = gate_pre.shape[0]
    tokens = n * rows
    width = gate_pre.shape[1]
    feats = activations.shape[1]
    cotangent_all = lax.all_gather(cotangent, "gy", axis=0, tiled=True)
    activations_all = lax.all_gather(activations, "gy", axis=0, tiled=True)

    def relative(whole):
        blocks = whole.reshape(n, rows, whole.shape[1])
        return jnp.concatenate(
            [
                lax.dynamic_index_in_dim(blocks, lax.rem(me - r + n, n), 0, keepdims=False)
                for r in range(n)
            ],
            axis=0,
        )

    cot = relative(cotangent_all)
    act = relative(activations_all)
    total = None
    gate_grad = jnp.zeros((feats, width), BF)
    up_grad = jnp.zeros((feats, width), BF)
    down_grad = jnp.zeros((width, feats), BF)
    chunks = chunks_of(width)
    partials = [
        lax.dot_general(
            cot,
            lax.slice_in_dim(down_weight, at, at + size, axis=0),
            over_cols,
            preferred_element_type=F32,
        ).reshape(n, rows, size)
        for at, size in chunks
    ]
    gates, sums = ([], [])
    for k, (at, size) in enumerate(chunks):
        gate = lax.slice_in_dim(gate_pre, at, at + size, axis=1)
        up = lax.slice_in_dim(up_pre, at, at + size, axis=1)
        if k == 1:
            gate, up = (after(gate, partials[1]), after(up, partials[1]))
        if k >= 2:
            gate, up = (after(gate, sums[k - 2]), after(up, sums[k - 2]))
        gates.append((line_gather(gate, "gx", n), line_gather(up, "gx", n)))

        def part(r, k=k):
            term = partials[k][(n - r) % n]
            return after(term, sums[k - 1]) if k and r in (1, n - 1) else term

        sums.append(line_scatter(part, "gx", n).astype(BF))
    for (at, size), (gate, up), own in zip(chunks, gates, sums):
        grad_hidden = line_gather(own, "gx", n)
        done = [swiglu_grads(*terms) for terms in zip(gate, up, grad_hidden)]
        hidden, grad_gate, grad_up = (jnp.concatenate(part, axis=0) for part in zip(*done))
        term = lax.dot_general(
            grad_gate,
            lax.slice_in_dim(gate_weight, at, at + size, axis=1),
            over_cols,
            preferred_element_type=F32,
        ) + lax.dot_general(
            grad_up,
            lax.slice_in_dim(up_weight, at, at + size, axis=1),
            over_cols,
            preferred_element_type=F32,
        )
        total = term if total is None else total + term
        down = lax.dot_general(hidden, cot, over_rows, preferred_element_type=F32).astype(BF)
        first = lax.dot_general(act, grad_gate, over_rows, preferred_element_type=F32).astype(BF)
        second = lax.dot_general(act, grad_up, over_rows, preferred_element_type=F32).astype(BF)
        down_grad = lax.dynamic_update_slice(down_grad, down, (at, 0))
        gate_grad = lax.dynamic_update_slice(gate_grad, first, (0, at))
        up_grad = lax.dynamic_update_slice(up_grad, second, (0, at))
    total = total.reshape(n, rows, feats)
    total = jnp.stack(
        [
            lax.dynamic_index_in_dim(total, lax.rem(me - j + n, n), 0, keepdims=False)
            for j in range(n)
        ]
    ).reshape(ny, tokens // ny, feats)
    share = pair_scatter(total, "gy", ny)
    if nz == 2:
        share = share + lax.ppermute(share.astype(BF), "gz", [(0, 1), (1, 0)]).astype(F32)
        input_grad = share.astype(BF)
    else:
        input_grad = lax.psum(share, "gz").astype(BF)
    return (input_grad, gate_grad, up_grad, down_grad)


def solution(mesh):
    in_specs = (
        P("gy", "gx"),
        P("gy", "gx"),
        P("gx", ("gy", "gz")),
        P("gx", ("gy", "gz")),
        P("gx", ("gy", "gz")),
        P("gx", ("gy", "gz")),
        P(("gy", "gz"), "gx"),
    )
    out_specs = (P("gy", "gx"), P("gx", ("gy", "gz")), P("gx", ("gy", "gz")), P(("gy", "gz"), "gx"))
    return jax.shard_map(shards, mesh=mesh, in_specs=in_specs, out_specs=out_specs, check_vma=False)
```

profile of v0, /device:TPU:0, one launch (start us, length us, event | category | flops | bytes accessed | tf_op | source)
XLA Modules:
  0.0 658.3 jit_solution(11141083498765120991)
XLA Ops:
  24.0 22.7 %all-gather.3.cloned.1.call-done = bf16[1024,2048]{1,0:T(8,128)(2,1)} async-done(((bf16[256,2048]{1,0:T(8,128)(2,1)}), bf16[1024,2048]{1,0:T(8,128)(2,1)}) %all-gather.3.cloned.1.call-update) | async-done | bytes 4194320 | tf_op jit(solution)/shard_map/all_gather | solution.py:91
  49.3 9.6 %fusion.13 = f32[1024,1280]{1,0:T(8,128)S(1)} fusion(bf16[3328,2048]{1,0:T(8,128)(2,1)} %param.13, bf16[256,2048]{1,0:T(8,128)(2,1)S(1)} %get-tuple-element.51, bf16[256,2048]{1,0:T(8,128)(2,1)S(1)} %get-tuple-element.52, bf16[256,2048]{1,0:T(8,128)(2,1)S(1)} %get-tuple-element.53, bf16[256,2048]{1,0:T(8,128)(2,1)S(1)} %get-tuple-element.50), kind=kOutput, calls=%fused_computation.21 | convolution fusion | flops 5385486336 | bytes 14680064 | tf_op jit(solution)/shard_map/dot_general | solution.py:112
  67.4 9.5 %collective-permute-done = bf16[256,1280]{1,0:T(8,128)(2,1)S(1)} collective-permute-done((bf16[256,1280]{1,0:T(8,128)(2,1)S(1)}, bf16[256,1280]{1,0:T(8,128)(2,1)S(1)}, u32[]{:S(2)}, u32[]{:S(2)}) %collective-permute-start) | collective-permute-done | bytes 655392 | tf_op jit(solution)/shard_map/ppermute | solution.py:46
  87.2 12.4 %collective-permute-done.16 = bf16[256,1280]{1,0:T(8,128)(2,1)} collective-permute-done((bf16[256,1280]{1,0:T(8,128)(2,1)}, bf16[256,1280]{1,0:T(8,128)(2,1)}, u32[]{:S(2)}, u32[]{:S(2)}) %collective-permute-start.16) | collective-permute-done | bytes 655392 | tf_op jit(solution)/shard_map/ppermute | solution.py:34
  111.0 8.1 %collective-permute-done.13 = bf16[256,1280]{1,0:T(8,128)(2,1)S(1)} collective-permute-done((bf16[256,1280]{1,0:T(8,128)(2,1)S(1)}, bf16[256,1280]{1,0:T(8,128)(2,1)S(1)}, u32[]{:S(2)}, u32[]{:S(2)}) %collective-permute-start.13) | collective-permute-done | bytes 655392 | tf_op jit(solution)/shard_map/ppermute | solution.py:34
  119.2 12.1 %collective-permute-done.17 = bf16[256,1280]{1,0:T(8,128)(2,1)S(1)} collective-permute-done((bf16[256,1280]{1,0:T(8,128)(2,1)}, bf16[256,1280]{1,0:T(8,128)(2,1)S(1)}, u32[]{:S(2)}, u32[]{:S(2)}) %collective-permute-start.17) | collective-permute-done | bytes 655392 | tf_op jit(solution)/shard_map/ppermute | solution.py:34
  139.8 10.5 %fusion.7 = f32[1024,1280]{1,0:T(8,128)} fusion(bf16[3328,2048]{1,0:T(8,128)(2,1)} %param.13, bf16[256,2048]{1,0:T(8,128)(2,1)S(1)} %copy-done.64, bf16[256,2048]{1,0:T(8,128)(2,1)S(1)} %copy-done.69, bf16[256,2048]{1,0:T(8,128)(2,1)S(1)} %copy-done.74, bf16[256,2048]{1,0:T(8,128)(2,1)S(1)} %copy-done.59), kind=kOutput, calls=%fused_computation.15 | convolution fusion | flops 5385486336 | bytes 14680064 | tf_op jit(solution)/shard_map/dot_general | solution.py:112
  235.7 8.4 %convolution_convert_fusion.1 = bf16[1280,2048]{1,0:T(8,128)(2,1)S(1)} fusion(bf16[256,1280]{1,0:T(8,128)(2,1)S(1)} %copy-done.104, bf16[256,1280]{1,0:T(8,128)(2,1)S(1)} %copy-done.103, bf16[256,1280]{1,0:T(8,128)(2,1)} %get-tuple-element.22, bf16[256,1280]{1,0:T(8,128)(2,1)} %get-tuple-element.54, bf16[256,2048]{1,0:T(8,128)(2,1)} %copy-done.63, ...), kind=kOutput, calls=%fused_computation.4 | convolution fusion | flops 5398593536 | bytes 12058624 | tf_op jit(solution)/shard_map/dot_general | solution.py:151
  244.1 8.4 %dynamic_update_slice.33 = bf16[3328,2048]{1,0:T(8,128)(2,1)} pad(bf16[1280,2048]{1,0:T(8,128)(2,1)S(1)} %convolution_convert_fusion.1, bf16[]{:T(256)} %constant.119.clone.1), padding=0_2048x0_0 | pad | bytes 18874370 | tf_op jit(solution)/shard_map/dynamic_update_slice | solution.py:154
  266.5 7.7 %collective-permute-done.65 = bf16[256,768]{1,0:T(8,128)(2,1)S(1)} collective-permute-done((bf16[256,768]{1,0:T(8,128)(2,1)S(1)}, bf16[256,768]{1,0:T(8,128)(2,1)S(1)}, u32[]{:S(2)}, u32[]{:S(2)}) %collective-permute-start.65) | collective-permute-done | bytes 393248 | tf_op jit(solution)/shard_map/ppermute | solution.py:34
  291.6 10.8 %collective-permute-done.8 = bf16[256,1280]{1,0:T(8,128)(2,1)} collective-permute-done((bf16[256,1280]{1,0:T(8,128)(2,1)}, bf16[256,1280]{1,0:T(8,128)(2,1)}, u32[]{:S(2)}, u32[]{:S(2)}) %collective-permute-start.8) | collective-permute-done | bytes 655392 | tf_op jit(solution)/shard_map/ppermute | solution.py:34
  306.9 9.5 %collective-permute-done.36 = bf16[256,1280]{1,0:T(8,128)(2,1)S(1)} collective-permute-done((bf16[256,1280]{1,0:T(8,128)(2,1)}, bf16[256,1280]{1,0:T(8,128)(2,1)S(1)}, u32[]{:S(2)}, u32[]{:S(2)}) %collective-permute-start.36) | collective-permute-done | bytes 655392 | tf_op jit(solution)/shard_map/ppermute | solution.py:34
  317.1 7.1 %collective-permute-done.40 = bf16[256,1280]{1,0:T(8,128)(2,1)S(1)} collective-permute-done((bf16[256,1280]{1,0:T(8,128)(2,1)S(1)}, bf16[256,1280]{1,0:T(8,128)(2,1)S(1)}, u32[]{:S(2)}, u32[]{:S(2)}) %collective-permute-start.40) | collective-permute-done | bytes 655392 | tf_op jit(solution)/shard_map/ppermute | solution.py:34
  336.5 11.4 %collective-permute-done.37 = bf16[256,1280]{1,0:T(8,128)(2,1)S(1)} collective-permute-done((bf16[256,1280]{1,0:T(8,128)(2,1)S(1)}, bf16[256,1280]{1,0:T(8,128)(2,1)S(1)}, u32[]{:S(2)}, u32[]{:S(2)}) %collective-permute-start.37) | collective-permute-done | bytes 655392 | tf_op jit(solution)/shard_map/ppermute | solution.py:34
  350.2 11.7 %collective-permute-done.41 = bf16[256,1280]{1,0:T(8,128)(2,1)S(1)} collective-permute-done((bf16[256,1280]{1,0:T(8,128)(2,1)S(1)}, bf16[256,1280]{1,0:T(8,128)(2,1)S(1)}, u32[]{:S(2)}, u32[]{:S(2)}) %collective-permute-start.41) | collective-permute-done | bytes 655392 | tf_op jit(solution)/shard_map/ppermute | solution.py:34
  363.4 9.3 %fusion = bf16[3328,2048]{1,0:T(8,128)(2,1)} fusion(bf16[3328,2048]{1,0:T(8,128)(2,1)} %dynamic_update_slice.33, bf16[256,1280]{1,0:T(8,128)(2,1)S(1)} %get-tuple-element.20, bf16[256,1280]{1,0:T(8,128)(2,1)S(1)} %get-tuple-element.18, bf16[256,1280]{1,0:T(8,128)(2,1)S(1)} %get-tuple-element.16, bf16[256,1280]{1,0:T(8,128)(2,1)} %get-tuple-element.56, ...), kind=kOutput, calls=%fused_computation.3 | convolution fusion | flops 5398593536 | bytes 12058624 | tf_op jit(solution)/shard_map/dot_general | solution.py:151
  396.6 10.5 %fusion.11 = f32[1024,2048]{1,0:T(8,128)} fusion(bf16[2048,3328]{1,0:T(8,128)(2,1)} %param.11, bf16[256,1280]{1,0:T(8,128)(2,1)} %get-tuple-element.68, bf16[256,1280]{1,0:T(8,128)(2,1)} %get-tuple-element.66, bf16[256,1280]{1,0:T(8,128)(2,1)} %get-tuple-element.64, bf16[256,1280]{1,0:T(8,128)(2,1)} %get-tuple-element.55), kind=kOutput, calls=%fused_computation.19 | convolution fusion | flops 5379194880 | bytes 16252928 | tf_op jit(solution)/shard_map/dot_general | solution.py:139
  408.3 12.1 %fusion.9 = f32[1024,2048]{1,0:T(8,128)} fusion(bf16[2048,3328]{1,0:T(8,128)(2,1)} %param.12, bf16[256,1280]{1,0:T(8,128)(2,1)S(1)} %copy-done.89, bf16[256,1280]{1,0:T(8,128)(2,1)S(1)} %copy-done.87, bf16[256,1280]{1,0:T(8,128)(2,1)S(1)} %copy-done.90, bf16[256,1280]{1,0:T(8,128)(2,1)S(1)} %copy-done.86), kind=kOutput, calls=%fused_computation.17 | convolution fusion | flops 5379194880 | bytes 16252928 | tf_op jit(solution)/shard_map/dot_general | solution.py:144
  428.4 8.2 %convolution_convert_fusion.5 = bf16[2048,1280]{1,0:T(8,128)(2,1)} fusion(bf16[256,1280]{1,0:T(8,128)(2,1)S(1)} %copy-done.100, bf16[256,1280]{1,0:T(8,128)(2,1)S(1)} %copy-done.92, bf16[256,1280]{1,0:T(8,128)(2,1)S(1)} %copy-done.101, bf16[256,1280]{1,0:T(8,128)(2,1)S(1)} %copy-done.105, bf16[256,2048]{1,0:T(8,128)(2,1)S(1)} %copy-done.80, ...), kind=kOutput, calls=%fused_computation.10 | convolution fusion | flops 5398593536 | bytes 12058624 | tf_op jit(solution)/shard_map/dot_general | solution.py:152
  440.4 10.2 %collective-permute-start.50 = (bf16[256,768]{1,0:T(8,128)(2,1)S(1)}, bf16[256,768]{1,0:T(8,128)(2,1)S(1)}, u32[]{:S(2)}, u32[]{:S(2)}) collective-permute-start(bf16[256,768]{1,0:T(8,128)(2,1)S(1)} %get-tuple-element.59), channel_id=1, source_target_pairs={{0,8},{8,16},{16,24},{1,9},{9,17},{17,25},{2,10},{10,18},{18,26},{... | collective-permute-start | bytes 1179656 | tf_op jit(solution)/shard_map/ppermute | solution.py:46
  461.1 7.1 %collective-permute-done.53 = bf16[256,768]{1,0:T(8,128)(2,1)S(1)} collective-permute-done((bf16[256,768]{1,0:T(8,128)(2,1)S(1)}, bf16[256,768]{1,0:T(8,128)(2,1)S(1)}, u32[]{:S(2)}, u32[]{:S(2)}) %collective-permute-start.53) | collective-permute-done | bytes 393248 | tf_op jit(solution)/shard_map/ppermute | solution.py:47
  479.9 12.5 %fusion.5 = f32[1024,2048]{1,0:T(8,128)} fusion(bf16[2048,3328]{1,0:T(8,128)(2,1)} %param.11, bf16[256,1280]{1,0:T(8,128)(2,1)S(1)} %get-tuple-element.74, bf16[256,1280]{1,0:T(8,128)(2,1)S(1)} %get-tuple-element.72, bf16[256,1280]{1,0:T(8,128)(2,1)S(1)} %get-tuple-element.70, bf16[256,1280]{1,0:T(8,128)(2,1)S(1)} %fusion.64), kind=kOutput, calls=%fused_computation.13 | convolution fusion | flops 5379194880 | bytes 16252928 | tf_op jit(solution)/shard_map/dot_general | solution.py:139
  494.5 12.1 %fusion.3 = f32[1024,2048]{1,0:T(8,128)} fusion(bf16[2048,3328]{1,0:T(8,128)(2,1)} %param.12, bf16[256,1280]{1,0:T(8,128)(2,1)S(1)} %get-tuple-element.73, bf16[256,1280]{1,0:T(8,128)(2,1)S(1)} %get-tuple-element.71, bf16[256,1280]{1,0:T(8,128)(2,1)S(1)} %get-tuple-element.69, bf16[256,1280]{1,0:T(8,128)(2,1)S(1)} %copy-done.88), kind=kOutput, calls=%fused_computation.11 | convolution fusion | flops 5379194880 | bytes 16252928 | tf_op jit(solution)/shard_map/dot_general | solution.py:144
  506.5 7.3 %collective-permute-done.56 = bf16[256,768]{1,0:T(8,128)(2,1)S(1)} collective-permute-done((bf16[256,768]{1,0:T(8,128)(2,1)S(1)}, bf16[256,768]{1,0:T(8,128)(2,1)S(1)}, u32[]{:S(2)}, u32[]{:S(2)}) %collective-permute-start.56) | collective-permute-done | bytes 393248 | tf_op jit(solution)/shard_map/ppermute | solution.py:34
  517.5 6.7 %collective-permute-done.57 = bf16[256,768]{1,0:T(8,128)(2,1)S(1)} collective-permute-done((bf16[256,768]{1,0:T(8,128)(2,1)S(1)}, bf16[256,768]{1,0:T(8,128)(2,1)S(1)}, u32[]{:S(2)}, u32[]{:S(2)}) %collective-permute-start.57) | collective-permute-done | bytes 393248 | tf_op jit(solution)/shard_map/ppermute | solution.py:34
  524.8 9.5 %fusion.19 = f32[1024,2048]{1,0:T(8,128)} fusion(bf16[2048,3328]{1,0:T(8,128)(2,1)} %param.11, bf16[256,768]{1,0:T(8,128)(2,1)S(1)} %get-tuple-element.80, bf16[256,768]{1,0:T(8,128)(2,1)S(1)} %get-tuple-element.78, bf16[256,768]{1,0:T(8,128)(2,1)S(1)} %get-tuple-element.76, bf16[256,768]{1,0:T(8,128)(2,1)S(1)} %fusion.134), kind=kOutput, calls=%fused_computation.34 | convolution fusion | flops 3227516928 | bytes 13107200 | tf_op jit(solution)/shard_map/dot_general | solution.py:139
  534.4 18.9 %add_add_fusion = f32[1024,2048]{1,0:T(8,128)} fusion(f32[1024,2048]{1,0:T(8,128)} %fusion.19, f32[1024,2048]{1,0:T(8,128)} %fusion.5, f32[1024,2048]{1,0:T(8,128)} %fusion.3, f32[1024,2048]{1,0:T(8,128)} %fusion.11, f32[1024,2048]{1,0:T(8,128)} %fusion.9, bf16[2048,3328]{1,0:T(8,128)(2,1)} %param.12, bf16[256,768]{1,0:T(8,128)(2,1)S(1)} %get-tuple-element.79, ...), kind=kOutput, calls=%fused_computation.1 | convolution fusion | flops 3238002688 | bytes 55050240 | tf_op jit(solution)/shard_map/dot_general | solution.py:144
  558.6 11.2 %convolution_convert_fusion.3 = bf16[2048,1280]{1,0:T(8,128)(2,1)} fusion(bf16[256,1280]{1,0:T(8,128)(2,1)} %get-tuple-element.67, bf16[256,1280]{1,0:T(8,128)(2,1)} %get-tuple-element.65, bf16[256,1280]{1,0:T(8,128)(2,1)} %get-tuple-element.63, bf16[256,1280]{1,0:T(8,128)(2,1)} %get-tuple-element.30, bf16[256,2048]{1,0:T(8,128)(2,1)} %get-tuple-element.47, ...), kind=kOutput, calls=%fused_computation.7 | convolution fusion | flops 5398593536 | bytes 12058624 | tf_op jit(solution)/shard_map/dot_general | solution.py:153
  587.7 10.7 %fusion.2 = bf16[2048,3328]{1,0:T(8,128)(2,1)} fusion(bf16[2048,3328]{1,0:T(8,128)(2,1)} %dynamic_update_slice.27, bf16[256,1280]{1,0:T(8,128)(2,1)} %copy-done.98, bf16[256,1280]{1,0:T(8,128)(2,1)} %copy-done.95, bf16[256,1280]{1,0:T(8,128)(2,1)} %copy-done.99, bf16[256,1280]{1,0:T(8,128)(2,1)} %copy-done.91, bf16[256,2048]{1,0:T(8,128)(2,1)} %get-tuple-element.47, ...), kind=kOutput, calls=%fused_computation.9 | convolution fusion | flops 5398593536 | bytes 12058624 | tf_op jit(solution)/shard_map/dot_general | solution.py:152
  600.1 10.4 %fusion.1 = bf16[2048,3328]{1,0:T(8,128)(2,1)} fusion(bf16[2048,3328]{1,0:T(8,128)(2,1)} %dynamic_update_slice.30, bf16[256,1280]{1,0:T(8,128)(2,1)} %copy-done.96, bf16[256,1280]{1,0:T(8,128)(2,1)} %copy-done.93, bf16[256,1280]{1,0:T(8,128)(2,1)} %copy-done.97, bf16[256,1280]{1,0:T(8,128)(2,1)} %get-tuple-element.32, bf16[256,2048]{1,0:T(8,128)(2,1)S(1)} %copy-done.81, ...), kind=kOutput, calls=%fused_computation.6 | convolution fusion | flops 5398593536 | bytes 12058624 | tf_op jit(solution)/shard_map/dot_general | solution.py:153
  610.5 14.3 %collective-permute-done.73 = bf16[1,256,2048]{2,1,0:T(8,128)(2,1)S(1)} collective-permute-done((bf16[1,256,2048]{2,1,0:T(8,128)(2,1)S(1)}, bf16[1,256,2048]{2,1,0:T(8,128)(2,1)S(1)}, u32[]{:S(2)}, u32[]{:S(2)}) %collective-permute-start.73) | collective-permute-done | bytes 1048608 | tf_op jit(solution)/shard_map/ppermute | solution.py:64
  637.4 12.4 %collective-permute-done.74 = bf16[256,2048]{1,0:T(8,128)(2,1)S(1)} collective-permute-done((bf16[256,2048]{1,0:T(8,128)(2,1)S(1)}, bf16[256,2048]{1,0:T(8,128)(2,1)S(1)}, u32[]{:S(2)}, u32[]{:S(2)}) %collective-permute-start.74) | collective-permute-done | bytes 1048608 | tf_op jit(solution)/shard_map/ppermute | solution.py:166
  (449 shorter events, 296.7 us)
Async XLA Ops:
  7.2 39.6 %all-gather.3.cloned.1.call-start = ((), (), s32[]{:S(2)}) async-start(), calls=%async_computation | async-start | bytes 5242880 | tf_op jit(solution)/shard_map/all_gather | solution.py:91
  7.9 192.8 %all-gather.5.cloned.1.call-start = ((), (), s32[]{:S(2)}) async-start(), calls=%async_computation.1 | async-start | bytes 5242880 | tf_op jit(solution)/shard_map/all_gather | solution.py:92
  9.1 53.4 %collective-permute-start.10 = (bf16[256,1280]{1,0:T(8,128)(2,1)S(1)}, bf16[256,1280]{1,0:T(8,128)(2,1)S(1)}, u32[]{:S(2)}, u32[]{:S(2)}) collective-permute-start(bf16[256,1280]{1,0:T(8,128)(2,1)S(1)} %slice.125), channel_id=1, source_target_pairs={{0,8},{8,16},{16,24},{1,9},{9,17},{17,25},{2,10},{10,18},{18,26},{... | collective-permute-start | bytes 1966088 | tf_op jit(solution)/shard_map/ppermute | solution.py:33
  14.1 50.7 %collective-permute-start.11 = (bf16[256,1280]{1,0:T(8,128)(2,1)S(1)}, bf16[256,1280]{1,0:T(8,128)(2,1)S(1)}, u32[]{:S(2)}, u32[]{:S(2)}) collective-permute-start(bf16[256,1280]{1,0:T(8,128)(2,1)S(1)} %slice.125), channel_id=1, source_target_pairs={{8,0},{16,8},{24,16},{9,1},{17,9},{25,17},{10,2},{18,10},{26,18},{... | collective-permute-start | bytes 1966088 | tf_op jit(solution)/shard_map/ppermute | solution.py:34
  17.3 45.9 %collective-permute-start.14 = (bf16[256,1280]{1,0:T(8,128)(2,1)}, bf16[256,1280]{1,0:T(8,128)(2,1)}, u32[]{:S(2)}, u32[]{:S(2)}) collective-permute-start(bf16[256,1280]{1,0:T(8,128)(2,1)} %slice.126), channel_id=1, source_target_pairs={{0,8},{8,16},{16,24},{1,9},{9,17},{17,25},{2,10},{10,18},{18,26},{... | collective-permute-start | bytes 1966088 | tf_op jit(solution)/shard_map/ppermute | solution.py:33
  22.7 43.4 %collective-permute-start.15 = (bf16[256,1280]{1,0:T(8,128)(2,1)}, bf16[256,1280]{1,0:T(8,128)(2,1)}, u32[]{:S(2)}, u32[]{:S(2)}) collective-permute-start(bf16[256,1280]{1,0:T(8,128)(2,1)} %slice.126), channel_id=1, source_target_pairs={{8,0},{16,8},{24,16},{9,1},{17,9},{25,17},{10,2},{18,10},{26,18},{... | collective-permute-start | bytes 1966088 | tf_op jit(solution)/shard_map/ppermute | solution.py:34
  66.1 33.5 %collective-permute-start.16 = (bf16[256,1280]{1,0:T(8,128)(2,1)}, bf16[256,1280]{1,0:T(8,128)(2,1)}, u32[]{:S(2)}, u32[]{:S(2)}) collective-permute-start(bf16[256,1280]{1,0:T(8,128)(2,1)} %collective-permute-done.15), channel_id=1, source_target_pairs={{8,0},{16,8},{9,1},{17,9},{10,2},{18,10},{11,3},{19,11},{12,4},{20... | collective-permute-start | bytes 1966088 | tf_op jit(solution)/shard_map/ppermute | solution.py:34
  76.9 26.8 %collective-permute-start.3 = (bf16[256,1280]{1,0:T(8,128)(2,1)S(1)}, bf16[256,1280]{1,0:T(8,128)(2,1)}, u32[]{:S(2)}, u32[]{:S(2)}) collective-permute-start(bf16[256,1280]{1,0:T(8,128)(2,1)S(1)} %get-tuple-element.45), channel_id=1, source_target_pairs={{24,16},{25,17},{26,18},{27,19},{28,20},{29,21},{30,22},{31,23}} | collective-permute-start | bytes 1966088 | tf_op jit(solution)/shard_map/ppermute | solution.py:47
  79.4 25.6 %collective-permute-start.1 = (bf16[256,1280]{1,0:T(8,128)(2,1)}, bf16[256,1280]{1,0:T(8,128)(2,1)}, u32[]{:S(2)}, u32[]{:S(2)}) collective-permute-start(bf16[256,1280]{1,0:T(8,128)(2,1)} %add_convert_fusion.7), channel_id=1, source_target_pairs={{0,8},{8,16},{1,9},{9,17},{2,10},{10,18},{3,11},{11,19},{4,12},{12... | collective-permute-start | bytes 1966088 | tf_op jit(solution)/shard_map/ppermute | solution.py:46
  103.7 27.6 %collective-permute-start.17 = (bf16[256,1280]{1,0:T(8,128)(2,1)}, bf16[256,1280]{1,0:T(8,128)(2,1)S(1)}, u32[]{:S(2)}, u32[]{:S(2)}) collective-permute-start(bf16[256,1280]{1,0:T(8,128)(2,1)} %collective-permute-done.16), channel_id=1, source_target_pairs={{8,0},{9,1},{10,2},{11,3},{12,4},{13,5},{14,6},{15,7}} | collective-permute-start | bytes 1966088 | tf_op jit(solution)/shard_map/ppermute | solution.py:34
  107.3 28.3 %collective-permute-start.4 = (bf16[256,1280]{1,0:T(8,128)(2,1)S(1)}, bf16[256,1280]{1,0:T(8,128)(2,1)S(1)}, u32[]{:S(2)}, u32[]{:S(2)}) collective-permute-start(bf16[256,1280]{1,0:T(8,128)(2,1)S(1)} %get-tuple-element.43), channel_id=1, source_target_pairs={{16,8},{24,16},{17,9},{25,17},{18,10},{26,18},{19,11},{27,19},{20,... | collective-permute-start | bytes 1966088 | tf_op jit(solution)/shard_map/ppermute | solution.py:47
  133.0 25.7 %collective-permute-start.2 = (bf16[256,1280]{1,0:T(8,128)(2,1)S(1)}, bf16[256,1280]{1,0:T(8,128)(2,1)S(1)}, u32[]{:S(2)}, u32[]{:S(2)}) collective-permute-start(bf16[256,1280]{1,0:T(8,128)(2,1)S(1)} %get-tuple-element.42), channel_id=1, source_target_pairs={{0,8},{8,16},{16,24},{1,9},{9,17},{17,25},{2,10},{10,18},{18,26},{... | collective-permute-start | bytes 1966088 | tf_op jit(solution)/shard_map/ppermute | solution.py:46
  171.2 28.2 %collective-permute-start.59 = (bf16[256,768]{1,0:T(8,128)(2,1)S(1)}, bf16[256,768]{1,0:T(8,128)(2,1)}, u32[]{:S(2)}, u32[]{:S(2)}) collective-permute-start(bf16[256,768]{1,0:T(8,128)(2,1)S(1)} %get-tuple-element.5), channel_id=1, source_target_pairs={{8,0},{16,8},{24,16},{9,1},{17,9},{25,17},{10,2},{18,10},{26,18},{... | collective-permute-start | bytes 1179656 | tf_op jit(solution)/shard_map/ppermute | solution.py:34
  172.5 32.7 %collective-permute-start.62 = (bf16[256,768]{1,0:T(8,128)(2,1)S(1)}, bf16[256,768]{1,0:T(8,128)(2,1)}, u32[]{:S(2)}, u32[]{:S(2)}) collective-permute-start(bf16[256,768]{1,0:T(8,128)(2,1)S(1)} %get-tuple-element.6), channel_id=1, source_target_pairs={{0,8},{8,16},{16,24},{1,9},{9,17},{17,25},{2,10},{10,18},{18,26},{... | collective-permute-start | bytes 1179656 | tf_op jit(solution)/shard_map/ppermute | solution.py:33
  177.9 28.2 %collective-permute-start.63 = (bf16[256,768]{1,0:T(8,128)(2,1)S(1)}, bf16[256,768]{1,0:T(8,128)(2,1)}, u32[]{:S(2)}, u32[]{:S(2)}) collective-permute-start(bf16[256,768]{1,0:T(8,128)(2,1)S(1)} %get-tuple-element.6), channel_id=1, source_target_pairs={{8,0},{16,8},{24,16},{9,1},{17,9},{25,17},{10,2},{18,10},{26,18},{... | collective-permute-start | bytes 1179656 | tf_op jit(solution)/shard_map/ppermute | solution.py:34
  219.5 39.5 %collective-permute-start.6 = (bf16[256,1280]{1,0:T(8,128)(2,1)S(1)}, bf16[256,1280]{1,0:T(8,128)(2,1)}, u32[]{:S(2)}, u32[]{:S(2)}) collective-permute-start(bf16[256,1280]{1,0:T(8,128)(2,1)S(1)} %copy-done.5), channel_id=1, source_target_pairs={{0,8},{8,16},{16,24},{1,9},{9,17},{17,25},{2,10},{10,18},{18,26},{... | collective-permute-start | bytes 1966088 | tf_op jit(solution)/shard_map/ppermute | solution.py:33
  225.4 38.2 %collective-permute-start.7 = (bf16[256,1280]{1,0:T(8,128)(2,1)S(1)}, bf16[256,1280]{1,0:T(8,128)(2,1)}, u32[]{:S(2)}, u32[]{:S(2)}) collective-permute-start(bf16[256,1280]{1,0:T(8,128)(2,1)S(1)} %copy-done.5), channel_id=1, source_target_pairs={{8,0},{16,8},{24,16},{9,1},{17,9},{25,17},{10,2},{18,10},{26,18},{... | collective-permute-start | bytes 1966088 | tf_op jit(solution)/shard_map/ppermute | solution.py:34
  226.7 49.0 %collective-permute-start.27 = (bf16[256,1280]{1,0:T(8,128)(2,1)}, bf16[256,1280]{1,0:T(8,128)(2,1)}, u32[]{:S(2)}, u32[]{:S(2)}) collective-permute-start(bf16[256,1280]{1,0:T(8,128)(2,1)} %get-tuple-element.41), channel_id=1, source_target_pairs={{24,16},{25,17},{26,18},{27,19},{28,20},{29,21},{30,22},{31,23}} | collective-permute-start | bytes 1966088 | tf_op jit(solution)/shard_map/ppermute | solution.py:47
  275.8 26.6 %collective-permute-start.8 = (bf16[256,1280]{1,0:T(8,128)(2,1)}, bf16[256,1280]{1,0:T(8,128)(2,1)}, u32[]{:S(2)}, u32[]{:S(2)}) collective-permute-start(bf16[256,1280]{1,0:T(8,128)(2,1)} %collective-permute-done.7), channel_id=1, source_target_pairs={{8,0},{16,8},{9,1},{17,9},{10,2},{18,10},{11,3},{19,11},{12,4},{20... | collective-permute-start | bytes 1966088 | tf_op jit(solution)/shard_map/ppermute | solution.py:34
  280.0 46.9 %collective-permute-start.25 = (bf16[256,1280]{1,0:T(8,128)(2,1)S(1)}, bf16[256,1280]{1,0:T(8,128)(2,1)S(1)}, u32[]{:S(2)}, u32[]{:S(2)}) collective-permute-start(bf16[256,1280]{1,0:T(8,128)(2,1)S(1)} %copy-done.94), channel_id=1, source_target_pairs={{0,8},{8,16},{1,9},{9,17},{2,10},{10,18},{3,11},{11,19},{4,12},{12... | collective-permute-start | bytes 1966088 | tf_op jit(solution)/shard_map/ppermute | solution.py:46
  289.0 27.4 %collective-permute-start.36 = (bf16[256,1280]{1,0:T(8,128)(2,1)}, bf16[256,1280]{1,0:T(8,128)(2,1)S(1)}, u32[]{:S(2)}, u32[]{:S(2)}) collective-permute-start(bf16[256,1280]{1,0:T(8,128)(2,1)} %collective-permute-done.35), channel_id=1, source_target_pairs={{8,0},{16,8},{9,1},{17,9},{10,2},{18,10},{11,3},{19,11},{12,4},{20... | collective-permute-start | bytes 1966088 | tf_op jit(solution)/shard_map/ppermute | solution.py:34
  290.3 33.9 %collective-permute-start.40 = (bf16[256,1280]{1,0:T(8,128)(2,1)S(1)}, bf16[256,1280]{1,0:T(8,128)(2,1)S(1)}, u32[]{:S(2)}, u32[]{:S(2)}) collective-permute-start(bf16[256,1280]{1,0:T(8,128)(2,1)S(1)} %collective-permute-done.39), channel_id=1, source_target_pairs={{8,0},{16,8},{9,1},{17,9},{10,2},{18,10},{11,3},{19,11},{12,4},{20... | collective-permute-start | bytes 1966088 | tf_op jit(solution)/shard_map/ppermute | solution.py:34
  302.4 25.7 %collective-permute-start.28 = (bf16[256,1280]{1,0:T(8,128)(2,1)S(1)}, bf16[256,1280]{1,0:T(8,128)(2,1)S(1)}, u32[]{:S(2)}, u32[]{:S(2)}) collective-permute-start(bf16[256,1280]{1,0:T(8,128)(2,1)S(1)} %add_convert_fusion.1), channel_id=1, source_target_pairs={{16,8},{24,16},{17,9},{25,17},{18,10},{26,18},{19,11},{27,19},{20,... | collective-permute-start | bytes 1966088 | tf_op jit(solution)/shard_map/ppermute | solution.py:47
  326.9 35.1 %collective-permute-start.41 = (bf16[256,1280]{1,0:T(8,128)(2,1)S(1)}, bf16[256,1280]{1,0:T(8,128)(2,1)S(1)}, u32[]{:S(2)}, u32[]{:S(2)}) collective-permute-start(bf16[256,1280]{1,0:T(8,128)(2,1)S(1)} %collective-permute-done.40), channel_id=1, source_target_pairs={{8,0},{9,1},{10,2},{11,3},{12,4},{13,5},{14,6},{15,7}} | collective-permute-start | bytes 1966088 | tf_op jit(solution)/shard_map/ppermute | solution.py:34
  328.2 44.6 %collective-permute-start.21 = (bf16[256,1280]{1,0:T(8,128)(2,1)}, bf16[256,1280]{1,0:T(8,128)(2,1)}, u32[]{:S(2)}, u32[]{:S(2)}) collective-permute-start(bf16[256,1280]{1,0:T(8,128)(2,1)} %collective-permute-done.18), channel_id=1, source_target_pairs={{16,24},{17,25},{18,26},{19,27},{20,28},{21,29},{22,30},{23,31}} | collective-permute-start | bytes 1966088 | tf_op jit(solution)/shard_map/ppermute | solution.py:33
  331.1 45.0 %collective-permute-start.9 = (bf16[256,1280]{1,0:T(8,128)(2,1)}, bf16[256,1280]{1,0:T(8,128)(2,1)}, u32[]{:S(2)}, u32[]{:S(2)}) collective-permute-start(bf16[256,1280]{1,0:T(8,128)(2,1)} %collective-permute-done.8), channel_id=1, source_target_pairs={{8,0},{9,1},{10,2},{11,3},{12,4},{13,5},{14,6},{15,7}} | collective-permute-start | bytes 1966088 | tf_op jit(solution)/shard_map/ppermute | solution.py:34
  332.4 50.8 %collective-permute-start.29 = (bf16[256,1280]{1,0:T(8,128)(2,1)}, bf16[256,1280]{1,0:T(8,128)(2,1)}, u32[]{:S(2)}, u32[]{:S(2)}) collective-permute-start(bf16[256,1280]{1,0:T(8,128)(2,1)} %get-tuple-element.39), channel_id=1, source_target_pairs={{8,0},{16,8},{24,16},{9,1},{17,9},{25,17},{10,2},{18,10},{26,18},{... | collective-permute-start | bytes 1966088 | tf_op jit(solution)/shard_map/ppermute | solution.py:47
  347.9 35.3 %collective-permute-start.26 = (bf16[256,1280]{1,0:T(8,128)(2,1)}, bf16[256,1280]{1,0:T(8,128)(2,1)}, u32[]{:S(2)}, u32[]{:S(2)}) collective-permute-start(bf16[256,1280]{1,0:T(8,128)(2,1)} %get-tuple-element.38), channel_id=1, source_target_pairs={{0,8},{8,16},{16,24},{1,9},{9,17},{17,25},{2,10},{10,18},{18,26},{... | collective-permute-start | bytes 1966088 | tf_op jit(solution)/shard_map/ppermute | solution.py:46
  439.0 29.3 %collective-permute-start.53 = (bf16[256,768]{1,0:T(8,128)(2,1)S(1)}, bf16[256,768]{1,0:T(8,128)(2,1)S(1)}, u32[]{:S(2)}, u32[]{:S(2)}) collective-permute-start(bf16[256,768]{1,0:T(8,128)(2,1)S(1)} %get-tuple-element.60), channel_id=1, source_target_pairs={{8,0},{16,8},{24,16},{9,1},{17,9},{25,17},{10,2},{18,10},{26,18},{... | collective-permute-start | bytes 1179656 | tf_op jit(solution)/shard_map/ppermute | solution.py:47
  440.4 27.8 %collective-permute-start.50 = (bf16[256,768]{1,0:T(8,128)(2,1)S(1)}, bf16[256,768]{1,0:T(8,128)(2,1)S(1)}, u32[]{:S(2)}, u32[]{:S(2)}) collective-permute-start(bf16[256,768]{1,0:T(8,128)(2,1)S(1)} %get-tuple-element.59), channel_id=1, source_target_pairs={{0,8},{8,16},{16,24},{1,9},{9,17},{17,25},{2,10},{10,18},{18,26},{... | collective-permute-start | bytes 1179656 | tf_op jit(solution)/shard_map/ppermute | solution.py:46
  558.5 39.9 %collective-permute-start.72 = (bf16[2,256,2048]{2,1,0:T(8,128)(2,1)S(1)}, bf16[2,256,2048]{2,1,0:T(8,128)(2,1)S(1)}, u32[]{:S(2)}, u32[]{:S(2)}) collective-permute-start(bf16[2,256,2048]{2,1,0:T(8,128)(2,1)S(1)} %fusion.37), channel_id=1, source_target_pairs={{0,2},{2,0},{4,6},{6,4},{1,3},{3,1},{5,7},{7,5},{8,10},{10,8},{12,... | collective-permute-start | bytes 6291464 | tf_op jit(solution)/shard_map/ppermute | solution.py:64
  599.5 25.4 %collective-permute-start.73 = (bf16[1,256,2048]{2,1,0:T(8,128)(2,1)S(1)}, bf16[1,256,2048]{2,1,0:T(8,128)(2,1)S(1)}, u32[]{:S(2)}, u32[]{:S(2)}) collective-permute-start(bf16[1,256,2048]{2,1,0:T(8,128)(2,1)S(1)} %dynamic-slice_convert_fusion.1), channel_id=1, source_target_pairs={{0,4},{2,6},{4,0},{6,2},{1,5},{3,7},{5,1},{7,3},{8,12},{10,14},{12... | collective-permute-start | bytes 3145736 | tf_op jit(solution)/shard_map/ppermute | solution.py:64
  (169 other events, 3112.8 us)
Sparse Core Ops, SparseCore 0:
  9.6 37.1 all-gather.2
  84.7 31.7 all-gather.4
where the time goes:
time: 668 us; the launch traced here: 658 us
  waiting for transfers between devices  201 us (30%)
  matrix products  175 us (26%)
  starting transfers between devices  147 us (22%)
  other arithmetic  66.6 us (10%)
  local copies, waits for them, and re-layouts  50.5 us (8%)
  between operations  18.3 us (3%)
    ppermute x27, waiting for transfers between devices, line_gather(): lax.ppermute(from_right, axis, [(i, i - 1) for i in range(1, n - s + 1)])  122 us
    ppermute x27, starting transfers between devices, line_gather(): lax.ppermute(from_left, axis, [(i, i + 1) for i in range(s - 1, n - 1)])  53 us
    ppermute x9, starting transfers between devices, line_scatter(): lax.ppermute(to_right.astype(BF), axis, [(i, i + 1) for i in range(min(t,...  45.5 us
    dot_general x3, matrix products, shards(): lax.dot_general(grad_up, lax.slice_in_dim(up_weight, at, at + size, axis=...  43 us
    ppermute x27, starting transfers between devices, line_gather(): lax.ppermute(from_right, axis, [(i, i - 1) for i in range(1, n - s + 1)])  35.5 us
    dot_general x3, matrix products, shards(): lax.dot_general(grad_gate, lax.slice_in_dim(gate_weight, at, at + size, a...  32.5 us
    dot_general x3, matrix products, shards(): lax.dot_general(act, grad_up, over_rows, preferred_element_type=F32)  26.9 us
    dot_general x3, matrix products, shards(): lax.dot_general(cot, lax.slice_in_dim(down_weight, at, at + size, axis=0)...  25.5 us
  transfers between devices with their start and end apart: 77, of which 25 were waited for; matrix products, arithmetic and copies ran while one was open for 37% of the time, Pallas kernels for 0%

commit v1 on v0

--- a/solution.py
+++ b/solution.py
@@ -88,8 +88,11 @@
     tokens = n * rows
     width = gate_pre.shape[1]
     feats = activations.shape[1]
-    cotangent_all = lax.all_gather(cotangent, "gy", axis=0, tiled=True)
-    activations_all = lax.all_gather(activations, "gy", axis=0, tiled=True)
+    cotangent_all, activations_all = jnp.split(
+        lax.all_gather(jnp.concatenate([cotangent, activations], axis=1), "gy", axis=0, tiled=True),
+        [cotangent.shape[1]],
+        1,
+    )
 
     def relative(whole):
         blocks = whole.reshape(n, rows, whole.shape[1])

time: 668 us -> 691 us (1.034)
  waiting for transfers between devices: 201 us -> 233 us
  starting transfers between devices: 147 us -> 140 us
    all_gather x2 -> x1, waiting for transfers between devices: 22.8 us -> 45.2 us  [shards(): lax.all_gather(jnp.concatenate([cotangent, activations], axis=1), 'gy', a...]
  transfers between devices with their start and end apart: 77 -> 76, of which waited for: 25 -> 26; matrix products, arithmetic and copies ran while one was open for 37% -> 35% of each run, Pallas kernels for 0% -> 0%
where the time goes in v1:
time: 691 us; the launch traced here: 682 us
  waiting for transfers between devices  233 us (34%)
  matrix products  177 us (26%)
  starting transfers between devices  140 us (20%)
  other arithmetic  61.8 us (9%)
  local copies, waits for them, and re-layouts  51.4 us (7%)
  between operations  18.5 us (3%)
    ppermute x27, waiting for transfers between devices, line_gather(): lax.ppermute(from_right, axis, [(i, i - 1) for i in range(1, n - s + 1)])  127 us
    ppermute x27, starting transfers between devices, line_gather(): lax.ppermute(from_left, axis, [(i, i + 1) for i in range(s - 1, n - 1)])  50.8 us
    all_gather x1, waiting for transfers between devices, shards(): lax.all_gather(jnp.concatenate([cotangent, activations], axis=1), 'gy', a...  45.2 us
    dot_general x3, matrix products, shards(): lax.dot_general(grad_up, lax.slice_in_dim(up_weight, at, at + size, axis=...  43.1 us
    ppermute x9, starting transfers between devices, line_scatter(): lax.ppermute(to_right.astype(BF), axis, [(i, i + 1) for i in range(min(t,...  40.6 us
    ppermute x27, starting transfers between devices, line_gather(): lax.ppermute(from_right, axis, [(i, i - 1) for i in range(1, n - s + 1)])  35.4 us
    dot_general x3, matrix products, shards(): lax.dot_general(grad_gate, lax.slice_in_dim(gate_weight, at, at + size, a...  32.4 us
    dot_general x3, matrix products, shards(): lax.dot_general(cot, lax.slice_in_dim(down_weight, at, at + size, axis=0)...  27.1 us
  transfers between devices with their start and end apart: 76, of which 26 were waited for; matrix products, arithmetic and copies ran while one was open for 35% of the time, Pallas kernels for 0%

profile of v1, /device:TPU:0, one launch (start us, length us, event | category | flops | bytes accessed | tf_op | source)
XLA Modules:
  0.0 681.5 jit_solution(2609010984559637225)
XLA Ops:
  26.4 45.2 %all-gather.2.cloned.1.call-done = bf16[1024,4096]{1,0:T(8,128)(2,1)} async-done(((bf16[256,4096]{1,0:T(8,128)(2,1)}), bf16[1024,4096]{1,0:T(8,128)(2,1)}) %all-gather.2.cloned.1.call-update) | async-done | bytes 8388624 | tf_op jit(solution)/shard_map/all_gather | solution.py:92
  77.5 9.6 %fusion.13 = f32[1024,1280]{1,0:T(8,128)S(1)} fusion(bf16[3328,2048]{1,0:T(8,128)(2,1)} %param.13, bf16[256,2048]{1,0:T(8,128)(2,1)S(1)} %get-tuple-element.53, bf16[256,2048]{1,0:T(8,128)(2,1)S(1)} %get-tuple-element.54, bf16[256,2048]{1,0:T(8,128)(2,1)S(1)} %get-tuple-element.55, bf16[256,2048]{1,0:T(8,128)(2,1)S(1)} %get-tuple-element.52), kind=kOutput, calls=%fused_computation.21 | convolution fusion | flops 5385486336 | bytes 14680064 | tf_op jit(solution)/shard_map/dot_general | solution.py:115
  96.5 9.5 %collective-permute-done = bf16[256,1280]{1,0:T(8,128)(2,1)S(1)} collective-permute-done((bf16[256,1280]{1,0:T(8,128)(2,1)S(1)}, bf16[256,1280]{1,0:T(8,128)(2,1)S(1)}, u32[]{:S(2)}, u32[]{:S(2)}) %collective-permute-start) | collective-permute-done | bytes 655392 | tf_op jit(solution)/shard_map/ppermute | solution.py:46
  116.4 12.4 %collective-permute-done.16 = bf16[256,1280]{1,0:T(8,128)(2,1)} collective-permute-done((bf16[256,1280]{1,0:T(8,128)(2,1)}, bf16[256,1280]{1,0:T(8,128)(2,1)}, u32[]{:S(2)}, u32[]{:S(2)}) %collective-permute-start.16) | collective-permute-done | bytes 655392 | tf_op jit(solution)/shard_map/ppermute | solution.py:34
  141.1 7.3 %collective-permute-done.13 = bf16[256,1280]{1,0:T(8,128)(2,1)S(1)} collective-permute-done((bf16[256,1280]{1,0:T(8,128)(2,1)}, bf16[256,1280]{1,0:T(8,128)(2,1)S(1)}, u32[]{:S(2)}, u32[]{:S(2)}) %collective-permute-start.13) | collective-permute-done | bytes 655392 | tf_op jit(solution)/shard_map/ppermute | solution.py:34
  148.5 12.1 %collective-permute-done.17 = bf16[256,1280]{1,0:T(8,128)(2,1)S(1)} collective-permute-done((bf16[256,1280]{1,0:T(8,128)(2,1)}, bf16[256,1280]{1,0:T(8,128)(2,1)S(1)}, u32[]{:S(2)}, u32[]{:S(2)}) %collective-permute-start.17) | collective-permute-done | bytes 655392 | tf_op jit(solution)/shard_map/ppermute | solution.py:34
  169.1 10.5 %fusion.7 = f32[1024,1280]{1,0:T(8,128)} fusion(bf16[3328,2048]{1,0:T(8,128)(2,1)} %param.13, bf16[256,2048]{1,0:T(8,128)(2,1)S(1)} %copy-done.63, bf16[256,2048]{1,0:T(8,128)(2,1)S(1)} %copy-done.68, bf16[256,2048]{1,0:T(8,128)(2,1)S(1)} %copy-done.73, bf16[256,2048]{1,0:T(8,128)(2,1)S(1)} %copy-done.59), kind=kOutput, calls=%fused_computation.15 | convolution fusion | flops 5385486336 | bytes 14680064 | tf_op jit(solution)/shard_map/dot_general | solution.py:115
  234.8 10.1 %collective-permute-done.34 = bf16[256,1280]{1,0:T(8,128)(2,1)S(1)} collective-permute-done((bf16[256,1280]{1,0:T(8,128)(2,1)S(1)}, bf16[256,1280]{1,0:T(8,128)(2,1)S(1)}, u32[]{:S(2)}, u32[]{:S(2)}) %collective-permute-start.34) | collective-permute-done | bytes 655392 | tf_op jit(solution)/shard_map/ppermute | solution.py:33
  262.7 8.3 %convolution_convert_fusion.1 = bf16[1280,2048]{1,0:T(8,128)(2,1)S(1)} fusion(bf16[256,1280]{1,0:T(8,128)(2,1)} %get-tuple-element.26, bf16[256,1280]{1,0:T(8,128)(2,1)} %get-tuple-element.24, bf16[256,1280]{1,0:T(8,128)(2,1)} %get-tuple-element.22, bf16[256,1280]{1,0:T(8,128)(2,1)} %get-tuple-element.56, bf16[256,2048]{1,0:T(8,128)(2,1)} %copy-done.62, ...), kind=kOutput, calls=%fused_computation.4 | convolution fusion | flops 5398593536 | bytes 12058624 | tf_op jit(solution)/shard_map/dot_general | solution.py:154
  271.1 8.4 %dynamic_update_slice.33 = bf16[3328,2048]{1,0:T(8,128)(2,1)} pad(bf16[1280,2048]{1,0:T(8,128)(2,1)S(1)} %convolution_convert_fusion.1, bf16[]{:T(256)} %constant.119.clone.1), padding=0_2048x0_0 | pad | bytes 18874370 | tf_op jit(solution)/shard_map/dynamic_update_slice | solution.py:157
  293.4 7.7 %collective-permute-done.65 = bf16[256,768]{1,0:T(8,128)(2,1)S(1)} collective-permute-done((bf16[256,768]{1,0:T(8,128)(2,1)}, bf16[256,768]{1,0:T(8,128)(2,1)S(1)}, u32[]{:S(2)}, u32[]{:S(2)}) %collective-permute-start.65) | collective-permute-done | bytes 393248 | tf_op jit(solution)/shard_map/ppermute | solution.py:34
  318.5 10.7 %collective-permute-done.8 = bf16[256,1280]{1,0:T(8,128)(2,1)S(1)} collective-permute-done((bf16[256,1280]{1,0:T(8,128)(2,1)}, bf16[256,1280]{1,0:T(8,128)(2,1)S(1)}, u32[]{:S(2)}, u32[]{:S(2)}) %collective-permute-start.8) | collective-permute-done | bytes 655392 | tf_op jit(solution)/shard_map/ppermute | solution.py:34
  333.7 9.5 %collective-permute-done.36 = bf16[256,1280]{1,0:T(8,128)(2,1)S(1)} collective-permute-done((bf16[256,1280]{1,0:T(8,128)(2,1)S(1)}, bf16[256,1280]{1,0:T(8,128)(2,1)S(1)}, u32[]{:S(2)}, u32[]{:S(2)}) %collective-permute-start.36) | collective-permute-done | bytes 655392 | tf_op jit(solution)/shard_map/ppermute | solution.py:34
  363.0 12.0 %collective-permute-done.37 = bf16[256,1280]{1,0:T(8,128)(2,1)S(1)} collective-permute-done((bf16[256,1280]{1,0:T(8,128)(2,1)S(1)}, bf16[256,1280]{1,0:T(8,128)(2,1)S(1)}, u32[]{:S(2)}, u32[]{:S(2)}) %collective-permute-start.37) | collective-permute-done | bytes 655392 | tf_op jit(solution)/shard_map/ppermute | solution.py:34
  376.5 12.6 %collective-permute-done.41 = bf16[256,1280]{1,0:T(8,128)(2,1)S(1)} collective-permute-done((bf16[256,1280]{1,0:T(8,128)(2,1)S(1)}, bf16[256,1280]{1,0:T(8,128)(2,1)S(1)}, u32[]{:S(2)}, u32[]{:S(2)}) %collective-permute-start.41) | collective-permute-done | bytes 655392 | tf_op jit(solution)/shard_map/ppermute | solution.py:34
  390.8 9.8 %fusion = bf16[3328,2048]{1,0:T(8,128)(2,1)} fusion(bf16[3328,2048]{1,0:T(8,128)(2,1)} %dynamic_update_slice.33, bf16[256,1280]{1,0:T(8,128)(2,1)S(1)} %copy-done.102, bf16[256,1280]{1,0:T(8,128)(2,1)S(1)} %copy-done.101, bf16[256,1280]{1,0:T(8,128)(2,1)} %get-tuple-element.16, bf16[256,1280]{1,0:T(8,128)(2,1)} %get-tuple-element.58, ...), kind=kOutput, calls=%fused_computation.3 | convolution fusion | flops 5398593536 | bytes 12058624 | tf_op jit(solution)/shard_map/dot_general | solution.py:154
  420.0 10.5 %fusion.11 = f32[1024,2048]{1,0:T(8,128)} fusion(bf16[2048,3328]{1,0:T(8,128)(2,1)} %param.11, bf16[256,1280]{1,0:T(8,128)(2,1)} %get-tuple-element.70, bf16[256,1280]{1,0:T(8,128)(2,1)} %get-tuple-element.68, bf16[256,1280]{1,0:T(8,128)(2,1)} %get-tuple-element.66, bf16[256,1280]{1,0:T(8,128)(2,1)} %get-tuple-element.57), kind=kOutput, calls=%fused_computation.19 | convolution fusion | flops 5379194880 | bytes 16252928 | tf_op jit(solution)/shard_map/dot_general | solution.py:142
  431.6 12.1 %fusion.9 = f32[1024,2048]{1,0:T(8,128)} fusion(bf16[2048,3328]{1,0:T(8,128)(2,1)} %param.12, bf16[256,1280]{1,0:T(8,128)(2,1)S(1)} %copy-done.87, bf16[256,1280]{1,0:T(8,128)(2,1)S(1)} %copy-done.85, bf16[256,1280]{1,0:T(8,128)(2,1)S(1)} %copy-done.88, bf16[256,1280]{1,0:T(8,128)(2,1)S(1)} %copy-done.84), kind=kOutput, calls=%fused_computation.17 | convolution fusion | flops 5379194880 | bytes 16252928 | tf_op jit(solution)/shard_map/dot_general | solution.py:147
  451.8 8.2 %convolution_convert_fusion.5 = bf16[2048,1280]{1,0:T(8,128)(2,1)} fusion(bf16[256,1280]{1,0:T(8,128)(2,1)S(1)} %copy-done.98, bf16[256,1280]{1,0:T(8,128)(2,1)S(1)} %copy-done.90, bf16[256,1280]{1,0:T(8,128)(2,1)S(1)} %copy-done.99, bf16[256,1280]{1,0:T(8,128)(2,1)S(1)} %copy-done.103, bf16[256,2048]{1,0:T(8,128)(2,1)S(1)} %copy-done.78, ...), kind=kOutput, calls=%fused_computation.10 | convolution fusion | flops 5398593536 | bytes 12058624 | tf_op jit(solution)/shard_map/dot_general | solution.py:155
  463.8 10.3 %collective-permute-start.50 = (bf16[256,768]{1,0:T(8,128)(2,1)S(1)}, bf16[256,768]{1,0:T(8,128)(2,1)S(1)}, u32[]{:S(2)}, u32[]{:S(2)}) collective-permute-start(bf16[256,768]{1,0:T(8,128)(2,1)S(1)} %get-tuple-element.61), channel_id=1, source_target_pairs={{0,8},{8,16},{16,24},{1,9},{9,17},{17,25},{2,10},{10,18},{18,26},{... | collective-permute-start | bytes 1179656 | tf_op jit(solution)/shard_map/ppermute | solution.py:46
  475.5 7.3 %collective-permute-done.32 = bf16[256,1280]{1,0:T(8,128)(2,1)S(1)} collective-permute-done((bf16[256,1280]{1,0:T(8,128)(2,1)S(1)}, bf16[256,1280]{1,0:T(8,128)(2,1)S(1)}, u32[]{:S(2)}, u32[]{:S(2)}) %collective-permute-start.32) | collective-permute-done | bytes 655392 | tf_op jit(solution)/shard_map/ppermute | solution.py:34
  502.1 12.4 %fusion.5 = f32[1024,2048]{1,0:T(8,128)} fusion(bf16[2048,3328]{1,0:T(8,128)(2,1)} %param.11, bf16[256,1280]{1,0:T(8,128)(2,1)S(1)} %get-tuple-element.76, bf16[256,1280]{1,0:T(8,128)(2,1)S(1)} %get-tuple-element.74, bf16[256,1280]{1,0:T(8,128)(2,1)S(1)} %get-tuple-element.72, bf16[256,1280]{1,0:T(8,128)(2,1)S(1)} %fusion.64), kind=kOutput, calls=%fused_computation.13 | convolution fusion | flops 5379194880 | bytes 16252928 | tf_op jit(solution)/shard_map/dot_general | solution.py:142
  516.7 12.1 %fusion.3 = f32[1024,2048]{1,0:T(8,128)} fusion(bf16[2048,3328]{1,0:T(8,128)(2,1)} %param.12, bf16[256,1280]{1,0:T(8,128)(2,1)S(1)} %get-tuple-element.75, bf16[256,1280]{1,0:T(8,128)(2,1)S(1)} %get-tuple-element.73, bf16[256,1280]{1,0:T(8,128)(2,1)S(1)} %get-tuple-element.71, bf16[256,1280]{1,0:T(8,128)(2,1)S(1)} %copy-done.86), kind=kOutput, calls=%fused_computation.11 | convolution fusion | flops 5379194880 | bytes 16252928 | tf_op jit(solution)/shard_map/dot_general | solution.py:147
  528.8 7.4 %collective-permute-done.56 = bf16[256,768]{1,0:T(8,128)(2,1)S(1)} collective-permute-done((bf16[256,768]{1,0:T(8,128)(2,1)S(1)}, bf16[256,768]{1,0:T(8,128)(2,1)S(1)}, u32[]{:S(2)}, u32[]{:S(2)}) %collective-permute-start.56) | collective-permute-done | bytes 393248 | tf_op jit(solution)/shard_map/ppermute | solution.py:34
  538.6 8.8 %collective-permute-done.57 = bf16[256,768]{1,0:T(8,128)(2,1)S(1)} collective-permute-done((bf16[256,768]{1,0:T(8,128)(2,1)S(1)}, bf16[256,768]{1,0:T(8,128)(2,1)S(1)}, u32[]{:S(2)}, u32[]{:S(2)}) %collective-permute-start.57) | collective-permute-done | bytes 393248 | tf_op jit(solution)/shard_map/ppermute | solution.py:34
  548.1 9.5 %fusion.19 = f32[1024,2048]{1,0:T(8,128)} fusion(bf16[2048,3328]{1,0:T(8,128)(2,1)} %param.11, bf16[256,768]{1,0:T(8,128)(2,1)S(1)} %get-tuple-element.82, bf16[256,768]{1,0:T(8,128)(2,1)S(1)} %get-tuple-element.80, bf16[256,768]{1,0:T(8,128)(2,1)S(1)} %get-tuple-element.78, bf16[256,768]{1,0:T(8,128)(2,1)S(1)} %fusion.134), kind=kOutput, calls=%fused_computation.34 | convolution fusion | flops 3227516928 | bytes 13107200 | tf_op jit(solution)/shard_map/dot_general | solution.py:142
  557.6 18.9 %add_add_fusion = f32[1024,2048]{1,0:T(8,128)} fusion(f32[1024,2048]{1,0:T(8,128)} %fusion.19, f32[1024,2048]{1,0:T(8,128)} %fusion.5, f32[1024,2048]{1,0:T(8,128)} %fusion.3, f32[1024,2048]{1,0:T(8,128)} %fusion.11, f32[1024,2048]{1,0:T(8,128)} %fusion.9, bf16[2048,3328]{1,0:T(8,128)(2,1)} %param.12, bf16[256,768]{1,0:T(8,128)(2,1)S(1)} %get-tuple-element.81, ...), kind=kOutput, calls=%fused_computation.1 | convolution fusion | flops 3238002688 | bytes 55050240 | tf_op jit(solution)/shard_map/dot_general | solution.py:147
  581.8 11.2 %convolution_convert_fusion.3 = bf16[2048,1280]{1,0:T(8,128)(2,1)} fusion(bf16[256,1280]{1,0:T(8,128)(2,1)} %get-tuple-element.69, bf16[256,1280]{1,0:T(8,128)(2,1)} %get-tuple-element.67, bf16[256,1280]{1,0:T(8,128)(2,1)} %get-tuple-element.65, bf16[256,1280]{1,0:T(8,128)(2,1)} %get-tuple-element.30, bf16[256,2048]{1,0:T(8,128)(2,1)} %get-tuple-element.49, ...), kind=kOutput, calls=%fused_computation.7 | convolution fusion | flops 5398593536 | bytes 12058624 | tf_op jit(solution)/shard_map/dot_general | solution.py:156
  610.9 10.7 %fusion.2 = bf16[2048,3328]{1,0:T(8,128)(2,1)} fusion(bf16[2048,3328]{1,0:T(8,128)(2,1)} %dynamic_update_slice.27, bf16[256,1280]{1,0:T(8,128)(2,1)} %copy-done.96, bf16[256,1280]{1,0:T(8,128)(2,1)} %copy-done.93, bf16[256,1280]{1,0:T(8,128)(2,1)} %copy-done.97, bf16[256,1280]{1,0:T(8,128)(2,1)} %copy-done.89, bf16[256,2048]{1,0:T(8,128)(2,1)} %get-tuple-element.49, ...), kind=kOutput, calls=%fused_computation.9 | convolution fusion | flops 5398593536 | bytes 12058624 | tf_op jit(solution)/shard_map/dot_general | solution.py:155
  623.3 10.4 %fusion.1 = bf16[2048,3328]{1,0:T(8,128)(2,1)} fusion(bf16[2048,3328]{1,0:T(8,128)(2,1)} %dynamic_update_slice.30, bf16[256,1280]{1,0:T(8,128)(2,1)} %copy-done.94, bf16[256,1280]{1,0:T(8,128)(2,1)} %copy-done.91, bf16[256,1280]{1,0:T(8,128)(2,1)} %copy-done.95, bf16[256,1280]{1,0:T(8,128)(2,1)} %get-tuple-element.32, bf16[256,2048]{1,0:T(8,128)(2,1)S(1)} %copy-done.79, ...), kind=kOutput, calls=%fused_computation.6 | convolution fusion | flops 5398593536 | bytes 12058624 | tf_op jit(solution)/shard_map/dot_general | solution.py:156
  633.7 14.3 %collective-permute-done.73 = bf16[1,256,2048]{2,1,0:T(8,128)(2,1)S(1)} collective-permute-done((bf16[1,256,2048]{2,1,0:T(8,128)(2,1)S(1)}, bf16[1,256,2048]{2,1,0:T(8,128)(2,1)S(1)}, u32[]{:S(2)}, u32[]{:S(2)}) %collective-permute-start.73) | collective-permute-done | bytes 1048608 | tf_op jit(solution)/shard_map/ppermute | solution.py:64
  660.6 12.4 %collective-permute-done.74 = bf16[256,2048]{1,0:T(8,128)(2,1)S(1)} collective-permute-done((bf16[256,2048]{1,0:T(8,128)(2,1)S(1)}, bf16[256,2048]{1,0:T(8,128)(2,1)S(1)}, u32[]{:S(2)}, u32[]{:S(2)}) %collective-permute-start.74) | collective-permute-done | bytes 1048608 | tf_op jit(solution)/shard_map/ppermute | solution.py:169
  (448 shorter events, 290.8 us)
Async XLA Ops:
  7.2 64.4 %all-gather.2.cloned.1.call-start = ((), (), s32[]{:S(2)}) async-start(), calls=%async_computation | async-start | bytes 10485760 | tf_op jit(solution)/shard_map/all_gather | solution.py:92
  12.5 79.1 %collective-permute-start.10 = (bf16[256,1280]{1,0:T(8,128)(2,1)}, bf16[256,1280]{1,0:T(8,128)(2,1)S(1)}, u32[]{:S(2)}, u32[]{:S(2)}) collective-permute-start(bf16[256,1280]{1,0:T(8,128)(2,1)} %slice.125), channel_id=1, source_target_pairs={{0,8},{8,16},{16,24},{1,9},{9,17},{17,25},{2,10},{10,18},{18,26},{... | collective-permute-start | bytes 1966088 | tf_op jit(solution)/shard_map/ppermute | solution.py:33
  17.4 76.5 %collective-permute-start.11 = (bf16[256,1280]{1,0:T(8,128)(2,1)}, bf16[256,1280]{1,0:T(8,128)(2,1)S(1)}, u32[]{:S(2)}, u32[]{:S(2)}) collective-permute-start(bf16[256,1280]{1,0:T(8,128)(2,1)} %slice.125), channel_id=1, source_target_pairs={{8,0},{16,8},{24,16},{9,1},{17,9},{25,17},{10,2},{18,10},{26,18},{... | collective-permute-start | bytes 1966088 | tf_op jit(solution)/shard_map/ppermute | solution.py:34
  19.7 72.7 %collective-permute-start.14 = (bf16[256,1280]{1,0:T(8,128)(2,1)}, bf16[256,1280]{1,0:T(8,128)(2,1)}, u32[]{:S(2)}, u32[]{:S(2)}) collective-permute-start(bf16[256,1280]{1,0:T(8,128)(2,1)} %slice.126), channel_id=1, source_target_pairs={{0,8},{8,16},{16,24},{1,9},{9,17},{17,25},{2,10},{10,18},{18,26},{... | collective-permute-start | bytes 1966088 | tf_op jit(solution)/shard_map/ppermute | solution.py:33
  25.1 70.2 %collective-permute-start.15 = (bf16[256,1280]{1,0:T(8,128)(2,1)}, bf16[256,1280]{1,0:T(8,128)(2,1)}, u32[]{:S(2)}, u32[]{:S(2)}) collective-permute-start(bf16[256,1280]{1,0:T(8,128)(2,1)} %slice.126), channel_id=1, source_target_pairs={{8,0},{16,8},{24,16},{9,1},{17,9},{25,17},{10,2},{18,10},{26,18},{... | collective-permute-start | bytes 1966088 | tf_op jit(solution)/shard_map/ppermute | solution.py:34
  95.2 33.5 %collective-permute-start.16 = (bf16[256,1280]{1,0:T(8,128)(2,1)}, bf16[256,1280]{1,0:T(8,128)(2,1)}, u32[]{:S(2)}, u32[]{:S(2)}) collective-permute-start(bf16[256,1280]{1,0:T(8,128)(2,1)} %collective-permute-done.15), channel_id=1, source_target_pairs={{8,0},{16,8},{9,1},{17,9},{10,2},{18,10},{11,3},{19,11},{12,4},{20... | collective-permute-start | bytes 1966088 | tf_op jit(solution)/shard_map/ppermute | solution.py:34
  106.0 27.0 %collective-permute-start.3 = (bf16[256,1280]{1,0:T(8,128)(2,1)}, bf16[256,1280]{1,0:T(8,128)(2,1)}, u32[]{:S(2)}, u32[]{:S(2)}) collective-permute-start(bf16[256,1280]{1,0:T(8,128)(2,1)} %get-tuple-element.47), channel_id=1, source_target_pairs={{24,16},{25,17},{26,18},{27,19},{28,20},{29,21},{30,22},{31,23}} | collective-permute-start | bytes 1966088 | tf_op jit(solution)/shard_map/ppermute | solution.py:47
  109.3 25.0 %collective-permute-start.1 = (bf16[256,1280]{1,0:T(8,128)(2,1)}, bf16[256,1280]{1,0:T(8,128)(2,1)}, u32[]{:S(2)}, u32[]{:S(2)}) collective-permute-start(bf16[256,1280]{1,0:T(8,128)(2,1)} %add_convert_fusion.7), channel_id=1, source_target_pairs={{0,8},{8,16},{1,9},{9,17},{2,10},{10,18},{3,11},{11,19},{4,12},{12... | collective-permute-start | bytes 1966088 | tf_op jit(solution)/shard_map/ppermute | solution.py:46
  133.0 27.7 %collective-permute-start.17 = (bf16[256,1280]{1,0:T(8,128)(2,1)}, bf16[256,1280]{1,0:T(8,128)(2,1)S(1)}, u32[]{:S(2)}, u32[]{:S(2)}) collective-permute-start(bf16[256,1280]{1,0:T(8,128)(2,1)} %collective-permute-done.16), channel_id=1, source_target_pairs={{8,0},{9,1},{10,2},{11,3},{12,4},{13,5},{14,6},{15,7}} | collective-permute-start | bytes 1966088 | tf_op jit(solution)/shard_map/ppermute | solution.py:34
  137.4 27.6 %collective-permute-start.4 = (bf16[256,1280]{1,0:T(8,128)(2,1)S(1)}, bf16[256,1280]{1,0:T(8,128)(2,1)S(1)}, u32[]{:S(2)}, u32[]{:S(2)}) collective-permute-start(bf16[256,1280]{1,0:T(8,128)(2,1)S(1)} %get-tuple-element.45), channel_id=1, source_target_pairs={{16,8},{24,16},{17,9},{25,17},{18,10},{26,18},{19,11},{27,19},{20,... | collective-permute-start | bytes 1966088 | tf_op jit(solution)/shard_map/ppermute | solution.py:47
  162.3 25.6 %collective-permute-start.2 = (bf16[256,1280]{1,0:T(8,128)(2,1)}, bf16[256,1280]{1,0:T(8,128)(2,1)S(1)}, u32[]{:S(2)}, u32[]{:S(2)}) collective-permute-start(bf16[256,1280]{1,0:T(8,128)(2,1)} %get-tuple-element.44), channel_id=1, source_target_pairs={{0,8},{8,16},{16,24},{1,9},{9,17},{17,25},{2,10},{10,18},{18,26},{... | collective-permute-start | bytes 1966088 | tf_op jit(solution)/shard_map/ppermute | solution.py:46
  202.3 25.1 %collective-permute-start.59 = (bf16[256,768]{1,0:T(8,128)(2,1)S(1)}, bf16[256,768]{1,0:T(8,128)(2,1)S(1)}, u32[]{:S(2)}, u32[]{:S(2)}) collective-permute-start(bf16[256,768]{1,0:T(8,128)(2,1)S(1)} %get-tuple-element.5), channel_id=1, source_target_pairs={{8,0},{16,8},{24,16},{9,1},{17,9},{25,17},{10,2},{18,10},{26,18},{... | collective-permute-start | bytes 1179656 | tf_op jit(solution)/shard_map/ppermute | solution.py:34
  203.6 27.3 %collective-permute-start.62 = (bf16[256,768]{1,0:T(8,128)(2,1)S(1)}, bf16[256,768]{1,0:T(8,128)(2,1)S(1)}, u32[]{:S(2)}, u32[]{:S(2)}) collective-permute-start(bf16[256,768]{1,0:T(8,128)(2,1)S(1)} %get-tuple-element.6), channel_id=1, source_target_pairs={{0,8},{8,16},{16,24},{1,9},{9,17},{17,25},{2,10},{10,18},{18,26},{... | collective-permute-start | bytes 1179656 | tf_op jit(solution)/shard_map/ppermute | solution.py:33
  218.5 26.5 %collective-permute-start.34 = (bf16[256,1280]{1,0:T(8,128)(2,1)S(1)}, bf16[256,1280]{1,0:T(8,128)(2,1)S(1)}, u32[]{:S(2)}, u32[]{:S(2)}) collective-permute-start(bf16[256,1280]{1,0:T(8,128)(2,1)S(1)} %get-tuple-element.59), channel_id=1, source_target_pairs={{0,8},{8,16},{16,24},{1,9},{9,17},{17,25},{2,10},{10,18},{18,26},{... | collective-permute-start | bytes 1966088 | tf_op jit(solution)/shard_map/ppermute | solution.py:33
  247.6 38.0 %collective-permute-start.6 = (bf16[256,1280]{1,0:T(8,128)(2,1)S(1)}, bf16[256,1280]{1,0:T(8,128)(2,1)}, u32[]{:S(2)}, u32[]{:S(2)}) collective-permute-start(bf16[256,1280]{1,0:T(8,128)(2,1)S(1)} %get-tuple-element.31), channel_id=1, source_target_pairs={{0,8},{8,16},{16,24},{1,9},{9,17},{17,25},{2,10},{10,18},{18,26},{... | collective-permute-start | bytes 1966088 | tf_op jit(solution)/shard_map/ppermute | solution.py:33
  253.4 36.8 %collective-permute-start.7 = (bf16[256,1280]{1,0:T(8,128)(2,1)S(1)}, bf16[256,1280]{1,0:T(8,128)(2,1)}, u32[]{:S(2)}, u32[]{:S(2)}) collective-permute-start(bf16[256,1280]{1,0:T(8,128)(2,1)S(1)} %get-tuple-element.31), channel_id=1, source_target_pairs={{8,0},{16,8},{24,16},{9,1},{17,9},{25,17},{10,2},{18,10},{26,18},{... | collective-permute-start | bytes 1966088 | tf_op jit(solution)/shard_map/ppermute | solution.py:34
  254.7 47.9 %collective-permute-start.27 = (bf16[256,1280]{1,0:T(8,128)(2,1)}, bf16[256,1280]{1,0:T(8,128)(2,1)}, u32[]{:S(2)}, u32[]{:S(2)}) collective-permute-start(bf16[256,1280]{1,0:T(8,128)(2,1)} %get-tuple-element.43), channel_id=1, source_target_pairs={{24,16},{25,17},{26,18},{27,19},{28,20},{29,21},{30,22},{31,23}} | collective-permute-start | bytes 1966088 | tf_op jit(solution)/shard_map/ppermute | solution.py:47
  302.6 26.6 %collective-permute-start.8 = (bf16[256,1280]{1,0:T(8,128)(2,1)}, bf16[256,1280]{1,0:T(8,128)(2,1)S(1)}, u32[]{:S(2)}, u32[]{:S(2)}) collective-permute-start(bf16[256,1280]{1,0:T(8,128)(2,1)} %collective-permute-done.7), channel_id=1, source_target_pairs={{8,0},{16,8},{9,1},{17,9},{10,2},{18,10},{11,3},{19,11},{12,4},{20... | collective-permute-start | bytes 1966088 | tf_op jit(solution)/shard_map/ppermute | solution.py:34
  306.8 47.3 %collective-permute-start.25 = (bf16[256,1280]{1,0:T(8,128)(2,1)S(1)}, bf16[256,1280]{1,0:T(8,128)(2,1)S(1)}, u32[]{:S(2)}, u32[]{:S(2)}) collective-permute-start(bf16[256,1280]{1,0:T(8,128)(2,1)S(1)} %copy-done.92), channel_id=1, source_target_pairs={{0,8},{8,16},{1,9},{9,17},{2,10},{10,18},{3,11},{11,19},{4,12},{12... | collective-permute-start | bytes 1966088 | tf_op jit(solution)/shard_map/ppermute | solution.py:46
  315.9 27.4 %collective-permute-start.36 = (bf16[256,1280]{1,0:T(8,128)(2,1)S(1)}, bf16[256,1280]{1,0:T(8,128)(2,1)S(1)}, u32[]{:S(2)}, u32[]{:S(2)}) collective-permute-start(bf16[256,1280]{1,0:T(8,128)(2,1)S(1)} %collective-permute-done.35), channel_id=1, source_target_pairs={{8,0},{16,8},{9,1},{17,9},{10,2},{18,10},{11,3},{19,11},{12,4},{20... | collective-permute-start | bytes 1966088 | tf_op jit(solution)/shard_map/ppermute | solution.py:34
  317.2 34.0 %collective-permute-start.40 = (bf16[256,1280]{1,0:T(8,128)(2,1)S(1)}, bf16[256,1280]{1,0:T(8,128)(2,1)S(1)}, u32[]{:S(2)}, u32[]{:S(2)}) collective-permute-start(bf16[256,1280]{1,0:T(8,128)(2,1)S(1)} %collective-permute-done.39), channel_id=1, source_target_pairs={{8,0},{16,8},{9,1},{17,9},{10,2},{18,10},{11,3},{19,11},{12,4},{20... | collective-permute-start | bytes 1966088 | tf_op jit(solution)/shard_map/ppermute | solution.py:34
  329.2 26.2 %collective-permute-start.28 = (bf16[256,1280]{1,0:T(8,128)(2,1)S(1)}, bf16[256,1280]{1,0:T(8,128)(2,1)S(1)}, u32[]{:S(2)}, u32[]{:S(2)}) collective-permute-start(bf16[256,1280]{1,0:T(8,128)(2,1)S(1)} %add_convert_fusion.1), channel_id=1, source_target_pairs={{16,8},{24,16},{17,9},{25,17},{18,10},{26,18},{19,11},{27,19},{20,... | collective-permute-start | bytes 1966088 | tf_op jit(solution)/shard_map/ppermute | solution.py:47
  333.0 25.4 %collective-permute-start.46 = (bf16[256,1280]{1,0:T(8,128)(2,1)S(1)}, bf16[256,1280]{1,0:T(8,128)(2,1)S(1)}, u32[]{:S(2)}, u32[]{:S(2)}) collective-permute-start(bf16[256,1280]{1,0:T(8,128)(2,1)S(1)} %collective-permute-done.43), channel_id=1, source_target_pairs={{16,24},{17,25},{18,26},{19,27},{20,28},{21,29},{22,30},{23,31}} | collective-permute-start | bytes 1966088 | tf_op jit(solution)/shard_map/ppermute | solution.py:33
  354.1 34.9 %collective-permute-start.41 = (bf16[256,1280]{1,0:T(8,128)(2,1)S(1)}, bf16[256,1280]{1,0:T(8,128)(2,1)S(1)}, u32[]{:S(2)}, u32[]{:S(2)}) collective-permute-start(bf16[256,1280]{1,0:T(8,128)(2,1)S(1)} %collective-permute-done.40), channel_id=1, source_target_pairs={{8,0},{9,1},{10,2},{11,3},{12,4},{13,5},{14,6},{15,7}} | collective-permute-start | bytes 1966088 | tf_op jit(solution)/shard_map/ppermute | solution.py:34
  355.4 45.2 %collective-permute-start.21 = (bf16[256,1280]{1,0:T(8,128)(2,1)}, bf16[256,1280]{1,0:T(8,128)(2,1)}, u32[]{:S(2)}, u32[]{:S(2)}) collective-permute-start(bf16[256,1280]{1,0:T(8,128)(2,1)} %collective-permute-done.18), channel_id=1, source_target_pairs={{16,24},{17,25},{18,26},{19,27},{20,28},{21,29},{22,30},{23,31}} | collective-permute-start | bytes 1966088 | tf_op jit(solution)/shard_map/ppermute | solution.py:33
  358.4 45.4 %collective-permute-start.9 = (bf16[256,1280]{1,0:T(8,128)(2,1)S(1)}, bf16[256,1280]{1,0:T(8,128)(2,1)}, u32[]{:S(2)}, u32[]{:S(2)}) collective-permute-start(bf16[256,1280]{1,0:T(8,128)(2,1)S(1)} %collective-permute-done.8), channel_id=1, source_target_pairs={{8,0},{9,1},{10,2},{11,3},{12,4},{13,5},{14,6},{15,7}} | collective-permute-start | bytes 1966088 | tf_op jit(solution)/shard_map/ppermute | solution.py:34
  359.8 51.8 %collective-permute-start.29 = (bf16[256,1280]{1,0:T(8,128)(2,1)}, bf16[256,1280]{1,0:T(8,128)(2,1)S(1)}, u32[]{:S(2)}, u32[]{:S(2)}) collective-permute-start(bf16[256,1280]{1,0:T(8,128)(2,1)} %get-tuple-element.41), channel_id=1, source_target_pairs={{8,0},{16,8},{24,16},{9,1},{17,9},{25,17},{10,2},{18,10},{26,18},{... | collective-permute-start | bytes 1966088 | tf_op jit(solution)/shard_map/ppermute | solution.py:47
  375.0 36.5 %collective-permute-start.26 = (bf16[256,1280]{1,0:T(8,128)(2,1)}, bf16[256,1280]{1,0:T(8,128)(2,1)S(1)}, u32[]{:S(2)}, u32[]{:S(2)}) collective-permute-start(bf16[256,1280]{1,0:T(8,128)(2,1)} %get-tuple-element.40), channel_id=1, source_target_pairs={{0,8},{8,16},{16,24},{1,9},{9,17},{17,25},{2,10},{10,18},{18,26},{... | collective-permute-start | bytes 1966088 | tf_op jit(solution)/shard_map/ppermute | solution.py:46
  462.3 29.0 %collective-permute-start.53 = (bf16[256,768]{1,0:T(8,128)(2,1)S(1)}, bf16[256,768]{1,0:T(8,128)(2,1)S(1)}, u32[]{:S(2)}, u32[]{:S(2)}) collective-permute-start(bf16[256,768]{1,0:T(8,128)(2,1)S(1)} %get-tuple-element.62), channel_id=1, source_target_pairs={{8,0},{16,8},{24,16},{9,1},{17,9},{25,17},{10,2},{18,10},{26,18},{... | collective-permute-start | bytes 1179656 | tf_op jit(solution)/shard_map/ppermute | solution.py:47
  463.8 27.5 %collective-permute-start.50 = (bf16[256,768]{1,0:T(8,128)(2,1)S(1)}, bf16[256,768]{1,0:T(8,128)(2,1)S(1)}, u32[]{:S(2)}, u32[]{:S(2)}) collective-permute-start(bf16[256,768]{1,0:T(8,128)(2,1)S(1)} %get-tuple-element.61), channel_id=1, source_target_pairs={{0,8},{8,16},{16,24},{1,9},{9,17},{17,25},{2,10},{10,18},{18,26},{... | collective-permute-start | bytes 1179656 | tf_op jit(solution)/shard_map/ppermute | solution.py:46
  581.7 39.9 %collective-permute-start.72 = (bf16[2,256,2048]{2,1,0:T(8,128)(2,1)S(1)}, bf16[2,256,2048]{2,1,0:T(8,128)(2,1)S(1)}, u32[]{:S(2)}, u32[]{:S(2)}) collective-permute-start(bf16[2,256,2048]{2,1,0:T(8,128)(2,1)S(1)} %fusion.37), channel_id=1, source_target_pairs={{0,2},{2,0},{4,6},{6,4},{1,3},{3,1},{5,7},{7,5},{8,10},{10,8},{12,... | collective-permute-start | bytes 6291464 | tf_op jit(solution)/shard_map/ppermute | solution.py:64
  622.6 25.4 %collective-permute-start.73 = (bf16[1,256,2048]{2,1,0:T(8,128)(2,1)S(1)}, bf16[1,256,2048]{2,1,0:T(8,128)(2,1)S(1)}, u32[]{:S(2)}, u32[]{:S(2)}) collective-permute-start(bf16[1,256,2048]{2,1,0:T(8,128)(2,1)S(1)} %dynamic-slice_convert_fusion.1), channel_id=1, source_target_pairs={{0,4},{2,6},{4,0},{6,2},{1,5},{3,7},{5,1},{7,3},{8,12},{10,14},{12... | collective-permute-start | bytes 3145736 | tf_op jit(solution)/shard_map/ppermute | solution.py:64
  (168 other events, 3186.2 us)
Sparse Core Ops, SparseCore 0:
  10.6 60.9 all-gather.1
